TPU v7x, 32 devices: a whole 2x2x4 slice. The times are simulated.
32 devices in a mesh: gx: 4 (over z), gy: 8 (over y, x, core).
Axes of the slice: x: 2, y: 2, z: 4, core: 2. Of those that a mesh axis runs over, the one named last changes fastest.
Arguments:
- right_side: float32 [16384, 128], P(('gx', 'gy')), may hold values from -6 to 6
- prec_diag: float32 [16384], P(('gx', 'gy')), may hold values from 3 to 6
- prec_values: float32 [8, 16384], P(None, ('gx', 'gy')), may hold values from -0.6 to 0.2
- prec_columns: int32 [8, 16384], P(None, ('gx', 'gy')), may hold values from 0 to 1023
- inverse: bfloat16 [32, 1024, 1024], P(('gx', 'gy')), may hold values from -1 to 1
- send_list: int32 [32, 4, 128], P(('gx', 'gy')), may hold values from 0 to 511, as said below
- send_count: int32 [32, 4], P(('gx', 'gy')), may hold values from 32 to 128, as said below
- own_weight: float32 [16384], P(('gx', 'gy')), may hold values from 0.2 to 5
- copy_weight: float32 [32, 4, 128], P(('gx', 'gy')), may hold values from 0.2 to 5
Outputs:
- solution: float32 [16384, 128], P(('gx', 'gy'))
- residual: float32 [16384, 128], P(('gx', 'gy'))
Inputs may be any that keep to these rules, and one draw needn't show every extreme that they name: `send_list`: the 128 entries of one subdomain and direction are distinct owned nodes. `send_count`: every subdomain has 128 live entries in at least one direction.
All inputs are finite; a program needn't handle non-finite values.
Results may differ from a plain program's by a relative error of at most 0.0072.
Values may be sent and summed in bfloat16 or wider, within the bound.
A program may use at most 64 MiB of HBM per device.

v0:
```python
import jax
import jax.numpy as jnp
from jax import lax
from jax.sharding import PartitionSpec as P

ITERS = 2


LOWER = 0.25
UPPER = 2.0


def with_halo(block, sides, width):
    for axis, dim in sides:
        count = lax.axis_size(axis)
        forward = [(i, i + 1) for i in range(count - 1)]
        backward = [(target, source) for source, target in forward]
        low = lax.ppermute(
            lax.slice_in_dim(block, block.shape[dim] - width, None, axis=dim), axis, forward
        )
        high = lax.ppermute(lax.slice_in_dim(block, 0, width, axis=dim), axis, backward)
        block = jnp.concatenate([low, block, high], axis=dim)
    return block


def side_live():
    row_place = lax.axis_index("gx")
    col_place = lax.axis_index("gy")
    return jnp.stack(
        [
            row_place > 0,
            row_place < lax.axis_size("gx") - 1,
            col_place > 0,
            col_place < lax.axis_size("gy") - 1,
        ]
    )


def pack_rows(vector, send_list, send_count):
    slot_ids = jnp.arange(send_list.shape[-1], dtype=jnp.int32)
    filled = slot_ids[None, :] < send_count[0][:, None]
    return jnp.where(filled[:, :, None], vector[send_list[0]], 0.0)


def from_sides(along_x, along_y):
    return jnp.stack([along_x[0], along_x[3], along_y[0], along_y[3]])


def fetch_ghosts(blocks):
    along_x = with_halo(blocks[0:2], (("gx", 0),), 1)
    along_y = with_halo(blocks[2:4], (("gy", 0),), 1)
    return from_sides(along_x, along_y)


def fetch_inputs(blocks):
    along_x = with_halo(blocks[0:2], (("gx", 0),), 1)
    along_y = with_halo(blocks[2:4], (("gy", 0),), 1)
    return from_sides(along_x, along_y)


def return_rows(blocks):
    along_x = with_halo(blocks[0:2], (("gx", 0),), 1)
    along_y = with_halo(blocks[2:4], (("gy", 0),), 1)
    return from_sides(along_x, along_y)


def precision_apply(vector, ghosts, prec_diag, prec_values, prec_columns):
    extended = jnp.concatenate([vector, ghosts.reshape(-1, vector.shape[1])], axis=0)
    coupled = prec_diag[:, None] * vector
    for entry in range(prec_values.shape[0]):
        coupled = coupled + prec_values[entry][:, None] * extended[prec_columns[entry]]
    return coupled


def precondition(vector, inverse, send_list, send_count, own_weight, slot_weight):
    owned_rows = vector.shape[0]
    width_here = vector.shape[1]
    matrix = inverse[0]
    blocks = pack_rows(vector, send_list, send_count).astype(jnp.bfloat16)
    owned_half = vector.astype(jnp.bfloat16)
    owned_term = jnp.dot(matrix[:, :owned_rows], owned_half, preferred_element_type=jnp.float32)
    ghosts = fetch_inputs(blocks).reshape(-1, width_here)
    result = owned_term + jnp.dot(
        matrix[:, owned_rows:], ghosts, preferred_element_type=jnp.float32
    )
    returned = return_rows(result[owned_rows:].reshape(4, -1, width_here))
    flat_list = send_list[0].reshape(-1)
    numerator = own_weight[:, None] * result[:owned_rows]
    numerator = numerator.at[flat_list].add(
        (slot_weight[:, :, None] * returned).reshape(-1, width_here)
    )
    denominator = own_weight.at[flat_list].add(slot_weight.reshape(-1))
    return numerator / denominator[:, None]


def per_device(
    right_side,
    prec_diag,
    prec_values,
    prec_columns,
    inverse,
    send_list,
    send_count,
    own_weight,
    copy_weight,
):
    slot_ids = jnp.arange(send_list.shape[-1], dtype=jnp.int32)
    inside = (slot_ids[None, :] < send_count[0][:, None]) & side_live()[:, None]
    slot_weight = jnp.where(inside, copy_weight[0], 0.0)
    center = 0.5 * (UPPER + LOWER)
    spread = 0.5 * (UPPER - LOWER)
    sigma_ratio = center / spread
    solution = jnp.zeros_like(right_side)
    residual = right_side
    direction = (
        precondition(residual, inverse, send_list, send_count, own_weight, slot_weight) / center
    )
    ratio_now = 1.0 / sigma_ratio
    for iteration in range(ITERS):
        solution = solution + direction
        ghosts = fetch_ghosts(pack_rows(direction, send_list, send_count))
        residual = residual - precision_apply(
            direction, ghosts, prec_diag, prec_values, prec_columns
        )
        if iteration < ITERS - 1:
            update = precondition(residual, inverse, send_list, send_count, own_weight, slot_weight)
            ratio_next = 1.0 / (2.0 * sigma_ratio - ratio_now)
            direction = ratio_next * ratio_now * direction + 2.0 * ratio_next / spread * update
            ratio_now = ratio_next
    return (solution, residual)


def solution(mesh):
    return jax.shard_map(
        per_device,
        mesh=mesh,
        in_specs=(
            P(("gx", "gy"), None),
            P(("gx", "gy")),
            P(None, ("gx", "gy")),
            P(None, ("gx", "gy")),
            P(("gx", "gy"), None, None),
            P(("gx", "gy"), None, None),
            P(("gx", "gy"), None),
            P(("gx", "gy")),
            P(("gx", "gy"), None, None),
        ),
        out_specs=(P(("gx", "gy"), None), P(("gx", "gy"), None)),
        check_vma=False,
    )
```

profile of v0, /device:TPU:1, one launch (start us, length us, event | category | flops | bytes accessed | tf_op | source)
XLA Modules:
  0.0 133.3 jit_solution(12227512481956933597)
XLA Ops:
  0.7 0.8 iota_compare_fusion
  1.4 0.7 fusion.10
  2.1 2.0 %gather_fusion = bf16[512,128]{1,0:T(8,128)(2,1)S(1)} fusion(f32[512,128]{1,0:T(8,128)} %param.9, s32[1024]{0:T(1024)S(1)} %pad_clamp_fusion.8), kind=kCustom, calls=%fused_computation | custom fusion | bytes 264192 | tf_op jit(solution)/shard_map/gather | solution.py:42
  4.3 4.0 %collective-permute-start = (bf16[1,128,128]{2,1,0:T(8,128)(2,1)S(1)}, bf16[1,128,128]{2,1,0:T(8,128)(2,1)S(1)}, u32[]{:S(2)}, u32[]{:S(2)}) collective-permute-start(bf16[1,128,128]{2,1,0:T(8,128)(2,1)S(1)} %get-tuple-element.24), channel_id=1, source_target_pairs={{0,8},{8,16},{16,24},{1,9},{9,17},{17,25},{2,10},{10,18},{18,26},{... | collective-permute-start | bytes 98312 | tf_op jit(solution)/shard_map/ppermute | solution.py:18
  8.3 2.9 %collective-permute-start.3 = (bf16[1,128,128]{2,1,0:T(8,128)(2,1)S(1)}, bf16[1,128,128]{2,1,0:T(8,128)(2,1)S(1)}, u32[]{:S(2)}, u32[]{:S(2)}) collective-permute-start(bf16[1,128,128]{2,1,0:T(8,128)(2,1)S(1)} %get-tuple-element.25), channel_id=1, source_target_pairs={{1,0},{2,1},{3,2},{4,3},{5,4},{6,5},{7,6},{9,8},{10,9},{11,10},{12... | collective-permute-start | bytes 98312 | tf_op jit(solution)/shard_map/ppermute | solution.py:21
  11.2 3.0 %collective-permute-start.2 = (bf16[1,128,128]{2,1,0:T(8,128)(2,1)S(1)}, bf16[1,128,128]{2,1,0:T(8,128)(2,1)S(1)}, u32[]{:S(2)}, u32[]{:S(2)}) collective-permute-start(bf16[1,128,128]{2,1,0:T(8,128)(2,1)S(1)} %get-tuple-element.26), channel_id=1, source_target_pairs={{0,1},{1,2},{2,3},{3,4},{4,5},{5,6},{6,7},{8,9},{9,10},{10,11},{11... | collective-permute-start | bytes 98312 | tf_op jit(solution)/shard_map/ppermute | solution.py:18
  14.2 1.3 collective-permute-start.1
  15.5 0.7 compare_select_fusion.8
  16.2 0.7 broadcast_multiply_fusion.1
  16.9 1.0 fusion.16
  17.9 1.0 compare_select_fusion.7
  19.1 1.7 %fusion.6 = f32[1024,128]{1,0:T(8,128)S(1)} fusion(bf16[1024,1024]{1,0:T(8,128)(2,1)} %bitcast.84, f32[512,128]{1,0:T(8,128)} %param.9), kind=kOutput, calls=%fused_computation.31 | convolution fusion | flops 134283264 | bytes 1835008 | tf_op jit(solution)/shard_map/dot_general | solution.py:81
  21.0 4.1 %scatter_fusion.1 = f32[512]{0:T(512)S(1)} fusion(f32[512]{0:T(512)S(1)} %copy.18, s32[512]{0:T(512)S(1)} %bitcast.96, f32[512]{0:T(512)S(1)} %bitcast_select_fusion), kind=kCustom, calls=%fused_computation.21 | custom fusion | flops 512 | bytes 8192 | tf_op jit(solution)/shard_map/scatter-add | solution.py:92
  25.6 4.0 %collective-permute-start.4 = (f32[1,128,128]{2,1,0:T(8,128)S(1)}, f32[1,128,128]{2,1,0:T(8,128)S(1)}, u32[]{:S(2)}, u32[]{:S(2)}) collective-permute-start(f32[1,128,128]{2,1,0:T(8,128)S(1)} %get-tuple-element.8), channel_id=1, source_target_pairs={{0,8},{8,16},{16,24},{1,9},{9,17},{17,25},{2,10},{10,18},{18,26},{... | collective-permute-start | bytes 196616 | tf_op jit(solution)/shard_map/ppermute | solution.py:18
  29.6 1.9 %collective-permute-start.7 = (f32[1,128,128]{2,1,0:T(8,128)S(1)}, f32[1,128,128]{2,1,0:T(8,128)S(1)}, u32[]{:S(2)}, u32[]{:S(2)}) collective-permute-start(f32[1,128,128]{2,1,0:T(8,128)S(1)} %get-tuple-element.9), channel_id=1, source_target_pairs={{1,0},{2,1},{3,2},{4,3},{5,4},{6,5},{7,6},{9,8},{10,9},{11,10},{12... | collective-permute-start | bytes 196616 | tf_op jit(solution)/shard_map/ppermute | solution.py:21
  31.5 3.6 %collective-permute-start.6 = (f32[1,128,128]{2,1,0:T(8,128)S(1)}, f32[1,128,128]{2,1,0:T(8,128)S(1)}, u32[]{:S(2)}, u32[]{:S(2)}) collective-permute-start(f32[1,128,128]{2,1,0:T(8,128)S(1)} %get-tuple-element.10), channel_id=1, source_target_pairs={{0,1},{1,2},{2,3},{3,4},{4,5},{5,6},{6,7},{8,9},{9,10},{10,11},{11... | collective-permute-start | bytes 196616 | tf_op jit(solution)/shard_map/ppermute | solution.py:18
  35.2 1.3 collective-permute-start.5
  36.6 3.5 %collective-permute-done.5 = f32[1,128,128]{2,1,0:T(8,128)S(1)} collective-permute-done((f32[1,128,128]{2,1,0:T(8,128)S(1)}, f32[1,128,128]{2,1,0:T(8,128)S(1)}, u32[]{:S(2)}, u32[]{:S(2)}) %collective-permute-start.5) | collective-permute-done | bytes 65568 | tf_op jit(solution)/shard_map/ppermute | solution.py:21
  40.3 3.4 %scatter_fusion = f32[512,128]{1,0:T(8,128)S(1)} fusion(f32[512,128]{1,0:T(8,128)S(1)} %slice_multiply_fusion.1, s32[512]{0:T(512)S(1)} %bitcast.97, f32[512,128]{1,0:T(8,128)S(1)} %bitcast_multiply_fusion.1), kind=kCustom, calls=%fused_computation.20 | custom fusion | flops 65536 | bytes 788480 | tf_op jit(solution)/shard_map/scatter-add | solution.py:89
  43.9 1.0 gather_fusion.1
  45.1 3.2 %collective-permute-start.8 = (f32[1,128,128]{2,1,0:T(8,128)S(1)}, f32[1,128,128]{2,1,0:T(8,128)S(1)}, u32[]{:S(2)}, u32[]{:S(2)}) collective-permute-start(f32[1,128,128]{2,1,0:T(8,128)S(1)} %get-tuple-element.16), channel_id=1, source_target_pairs={{0,8},{8,16},{16,24},{1,9},{9,17},{17,25},{2,10},{10,18},{18,26},{... | collective-permute-start | bytes 196616 | tf_op jit(solution)/shard_map/ppermute | solution.py:18
  48.3 2.1 %collective-permute-start.11 = (f32[1,128,128]{2,1,0:T(8,128)S(1)}, f32[1,128,128]{2,1,0:T(8,128)S(1)}, u32[]{:S(2)}, u32[]{:S(2)}) collective-permute-start(f32[1,128,128]{2,1,0:T(8,128)S(1)} %get-tuple-element.17), channel_id=1, source_target_pairs={{1,0},{2,1},{3,2},{4,3},{5,4},{6,5},{7,6},{9,8},{10,9},{11,10},{12... | collective-permute-start | bytes 196616 | tf_op jit(solution)/shard_map/ppermute | solution.py:21
  50.5 3.6 %collective-permute-start.10 = (f32[1,128,128]{2,1,0:T(8,128)S(1)}, f32[1,128,128]{2,1,0:T(8,128)S(1)}, u32[]{:S(2)}, u32[]{:S(2)}) collective-permute-start(f32[1,128,128]{2,1,0:T(8,128)S(1)} %get-tuple-element.18), channel_id=1, source_target_pairs={{0,1},{1,2},{2,3},{3,4},{4,5},{5,6},{6,7},{8,9},{9,10},{10,11},{11... | collective-permute-start | bytes 196616 | tf_op jit(solution)/shard_map/ppermute | solution.py:18
  54.1 1.3 collective-permute-start.9
  55.4 3.7 %collective-permute-done.9 = f32[1,128,128]{2,1,0:T(8,128)S(1)} collective-permute-done((f32[1,128,128]{2,1,0:T(8,128)S(1)}, f32[1,128,128]{2,1,0:T(8,128)S(1)}, u32[]{:S(2)}, u32[]{:S(2)}) %collective-permute-start.9) | collective-permute-done | bytes 65568 | tf_op jit(solution)/shard_map/ppermute | solution.py:21
  59.1 1.6 %gather_fusion.9 = f32[512,128]{1,0:T(8,128)} fusion(f32[1024,128]{1,0:T(8,128)S(1)} %pad_maximum_fusion, s32[1024]{0:T(1024)S(1)} %pad_clamp_fusion), kind=kCustom, calls=%fused_computation.9 | custom fusion | bytes 526336 | tf_op jit(solution)/shard_map/gather | solution.py:71
  60.8 1.6 %gather_fusion.8 = f32[512,128]{1,0:T(8,128)} fusion(f32[1024,128]{1,0:T(8,128)S(1)} %pad_maximum_fusion, s32[1024]{0:T(1024)S(1)} %pad_clamp_fusion.1), kind=kCustom, calls=%fused_computation.8 | custom fusion | bytes 526336 | tf_op jit(solution)/shard_map/gather | solution.py:71
  62.4 1.6 %gather_fusion.7 = f32[512,128]{1,0:T(8,128)} fusion(f32[1024,128]{1,0:T(8,128)S(1)} %pad_maximum_fusion, s32[1024]{0:T(1024)S(1)} %pad_clamp_fusion.2), kind=kCustom, calls=%fused_computation.7 | custom fusion | bytes 526336 | tf_op jit(solution)/shard_map/gather | solution.py:71
  64.1 1.6 %gather_fusion.6 = f32[512,128]{1,0:T(8,128)} fusion(f32[1024,128]{1,0:T(8,128)S(1)} %pad_maximum_fusion, s32[1024]{0:T(1024)S(1)} %pad_clamp_fusion.3), kind=kCustom, calls=%fused_computation.6 | custom fusion | bytes 526336 | tf_op jit(solution)/shard_map/gather | solution.py:71
  65.7 1.6 %gather_fusion.5 = f32[512,128]{1,0:T(8,128)} fusion(f32[1024,128]{1,0:T(8,128)S(1)} %pad_maximum_fusion, s32[1024]{0:T(1024)S(1)} %pad_clamp_fusion.4), kind=kCustom, calls=%fused_computation.5 | custom fusion | bytes 526336 | tf_op jit(solution)/shard_map/gather | solution.py:71
  67.4 1.6 %gather_fusion.4 = f32[512,128]{1,0:T(8,128)} fusion(f32[1024,128]{1,0:T(8,128)S(1)} %pad_maximum_fusion, s32[1024]{0:T(1024)S(1)} %pad_clamp_fusion.5), kind=kCustom, calls=%fused_computation.4 | custom fusion | bytes 526336 | tf_op jit(solution)/shard_map/gather | solution.py:71
  69.0 1.6 %gather_fusion.3 = f32[512,128]{1,0:T(8,128)} fusion(f32[1024,128]{1,0:T(8,128)S(1)} %pad_maximum_fusion, s32[1024]{0:T(1024)S(1)} %pad_clamp_fusion.6), kind=kCustom, calls=%fused_computation.3 | custom fusion | bytes 526336 | tf_op jit(solution)/shard_map/gather | solution.py:71
  70.6 1.7 %gather_fusion.2 = f32[512,128]{1,0:T(8,128)} fusion(f32[1024,128]{1,0:T(8,128)S(1)} %pad_maximum_fusion, s32[1024]{0:T(1024)S(1)} %pad_clamp_fusion.7), kind=kCustom, calls=%fused_computation.2 | custom fusion | bytes 526336 | tf_op jit(solution)/shard_map/gather | solution.py:71
  72.3 2.2 %add_subtract_fusion.1 = f32[512,128]{1,0:T(8,128)S(1)} fusion(f32[512,128]{1,0:T(8,128)S(1)} %copy-done, f32[512,128]{1,0:T(8,128)} %gather_fusion.9, f32[512,128]{1,0:T(8,128)} %gather_fusion.8, f32[512,128]{1,0:T(8,128)} %gather_fusion.7, f32[512,128]{1,0:T(8,128)} %gather_fusion.6, f32[512,128]{1,0:T(8,128)} %gather_fusion.5, ...), kind=kLoop, calls=%fused_computation.46 | loop fusion | flops 1245184 | bytes 2904064 | tf_op jit(solution)/shard_map/sub | solution.py:122
  74.5 1.1 gather_fusion.10
  75.8 3.2 %collective-permute-start.12 = (bf16[1,128,128]{2,1,0:T(8,128)(2,1)S(1)}, bf16[1,128,128]{2,1,0:T(8,128)(2,1)S(1)}, u32[]{:S(2)}, u32[]{:S(2)}) collective-permute-start(bf16[1,128,128]{2,1,0:T(8,128)(2,1)S(1)} %get-tuple-element.20), channel_id=1, source_target_pairs={{0,8},{8,16},{16,24},{1,9},{9,17},{17,25},{2,10},{10,18},{18,26},{... | collective-permute-start | bytes 98312 | tf_op jit(solution)/shard_map/ppermute | solution.py:18
  79.0 2.2 %collective-permute-start.15 = (bf16[1,128,128]{2,1,0:T(8,128)(2,1)S(1)}, bf16[1,128,128]{2,1,0:T(8,128)(2,1)S(1)}, u32[]{:S(2)}, u32[]{:S(2)}) collective-permute-start(bf16[1,128,128]{2,1,0:T(8,128)(2,1)S(1)} %get-tuple-element.21), channel_id=1, source_target_pairs={{1,0},{2,1},{3,2},{4,3},{5,4},{6,5},{7,6},{9,8},{10,9},{11,10},{12... | collective-permute-start | bytes 98312 | tf_op jit(solution)/shard_map/ppermute | solution.py:21
  81.1 4.3 %collective-permute-start.14 = (bf16[1,128,128]{2,1,0:T(8,128)(2,1)S(1)}, bf16[1,128,128]{2,1,0:T(8,128)(2,1)S(1)}, u32[]{:S(2)}, u32[]{:S(2)}) collective-permute-start(bf16[1,128,128]{2,1,0:T(8,128)(2,1)S(1)} %get-tuple-element.22), channel_id=1, source_target_pairs={{0,1},{1,2},{2,3},{3,4},{4,5},{5,6},{6,7},{8,9},{9,10},{10,11},{11... | collective-permute-start | bytes 98312 | tf_op jit(solution)/shard_map/ppermute | solution.py:18
  85.5 1.3 collective-permute-start.13
  86.8 0.4 fusion.4
  87.2 2.9 %collective-permute-done.13 = bf16[1,128,128]{2,1,0:T(8,128)(2,1)S(1)} collective-permute-done((bf16[1,128,128]{2,1,0:T(8,128)(2,1)S(1)}, bf16[1,128,128]{2,1,0:T(8,128)(2,1)S(1)}, u32[]{:S(2)}, u32[]{:S(2)}) %collective-permute-start.13) | collective-permute-done | bytes 32800 | tf_op jit(solution)/shard_map/ppermute | solution.py:21
  90.1 0.4 fusion
  90.6 1.9 %collective-permute-start.16 = (f32[1,128,128]{2,1,0:T(8,128)S(1)}, f32[1,128,128]{2,1,0:T(8,128)S(1)}, u32[]{:S(2)}, u32[]{:S(2)}) collective-permute-start(f32[1,128,128]{2,1,0:T(8,128)S(1)} %get-tuple-element.4), channel_id=1, source_target_pairs={{0,8},{8,16},{16,24},{1,9},{9,17},{17,25},{2,10},{10,18},{18,26},{... | collective-permute-start | bytes 196616 | tf_op jit(solution)/shard_map/ppermute | solution.py:18
  92.5 1.9 %collective-permute-start.19 = (f32[1,128,128]{2,1,0:T(8,128)S(1)}, f32[1,128,128]{2,1,0:T(8,128)S(1)}, u32[]{:S(2)}, u32[]{:S(2)}) collective-permute-start(f32[1,128,128]{2,1,0:T(8,128)S(1)} %get-tuple-element.5), channel_id=1, source_target_pairs={{1,0},{2,1},{3,2},{4,3},{5,4},{6,5},{7,6},{9,8},{10,9},{11,10},{12... | collective-permute-start | bytes 196616 | tf_op jit(solution)/shard_map/ppermute | solution.py:21
  94.5 4.5 %collective-permute-start.18 = (f32[1,128,128]{2,1,0:T(8,128)S(1)}, f32[1,128,128]{2,1,0:T(8,128)S(1)}, u32[]{:S(2)}, u32[]{:S(2)}) collective-permute-start(f32[1,128,128]{2,1,0:T(8,128)S(1)} %get-tuple-element.6), channel_id=1, source_target_pairs={{0,1},{1,2},{2,3},{3,4},{4,5},{5,6},{6,7},{8,9},{9,10},{10,11},{11... | collective-permute-start | bytes 196616 | tf_op jit(solution)/shard_map/ppermute | solution.py:18
  99.0 1.3 collective-permute-start.17
  100.5 3.5 %collective-permute-done.17 = f32[1,128,128]{2,1,0:T(8,128)S(1)} collective-permute-done((f32[1,128,128]{2,1,0:T(8,128)S(1)}, f32[1,128,128]{2,1,0:T(8,128)S(1)}, u32[]{:S(2)}, u32[]{:S(2)}) %collective-permute-start.17) | collective-permute-done | bytes 65568 | tf_op jit(solution)/shard_map/ppermute | solution.py:21
  104.2 3.6 %scatter_fusion.2 = f32[512,128]{1,0:T(8,128)S(1)} fusion(f32[512,128]{1,0:T(8,128)S(1)} %slice_multiply_fusion, s32[512]{0:T(512)S(1)} %bitcast.98, f32[512,128]{1,0:T(8,128)S(1)} %bitcast_multiply_fusion), kind=kCustom, calls=%fused_computation.22 | custom fusion | flops 65536 | bytes 788480 | tf_op jit(solution)/shard_map/scatter-add | solution.py:89
  107.8 0.9 fusion.11
  108.6 1.0 gather_fusion.11
  109.8 1.9 %collective-permute-start.20 = (f32[1,128,128]{2,1,0:T(8,128)S(1)}, f32[1,128,128]{2,1,0:T(8,128)S(1)}, u32[]{:S(2)}, u32[]{:S(2)}) collective-permute-start(f32[1,128,128]{2,1,0:T(8,128)S(1)} %get-tuple-element.12), channel_id=1, source_target_pairs={{0,8},{8,16},{16,24},{1,9},{9,17},{17,25},{2,10},{10,18},{18,26},{... | collective-permute-start | bytes 196616 | tf_op jit(solution)/shard_map/ppermute | solution.py:18
  111.8 1.9 %collective-permute-start.23 = (f32[1,128,128]{2,1,0:T(8,128)S(1)}, f32[1,128,128]{2,1,0:T(8,128)S(1)}, u32[]{:S(2)}, u32[]{:S(2)}) collective-permute-start(f32[1,128,128]{2,1,0:T(8,128)S(1)} %get-tuple-element.13), channel_id=1, source_target_pairs={{1,0},{2,1},{3,2},{4,3},{5,4},{6,5},{7,6},{9,8},{10,9},{11,10},{12... | collective-permute-start | bytes 196616 | tf_op jit(solution)/shard_map/ppermute | solution.py:21
  113.7 4.5 %collective-permute-start.22 = (f32[1,128,128]{2,1,0:T(8,128)S(1)}, f32[1,128,128]{2,1,0:T(8,128)S(1)}, u32[]{:S(2)}, u32[]{:S(2)}) collective-permute-start(f32[1,128,128]{2,1,0:T(8,128)S(1)} %get-tuple-element.14), channel_id=1, source_target_pairs={{0,1},{1,2},{2,3},{3,4},{4,5},{5,6},{6,7},{8,9},{9,10},{10,11},{11... | collective-permute-start | bytes 196616 | tf_op jit(solution)/shard_map/ppermute | solution.py:18
  118.3 1.3 collective-permute-start.21
  119.6 3.7 %collective-permute-done.21 = f32[1,128,128]{2,1,0:T(8,128)S(1)} collective-permute-done((f32[1,128,128]{2,1,0:T(8,128)S(1)}, f32[1,128,128]{2,1,0:T(8,128)S(1)}, u32[]{:S(2)}, u32[]{:S(2)}) %collective-permute-start.21) | collective-permute-done | bytes 65568 | tf_op jit(solution)/shard_map/ppermute | solution.py:21
  123.3 1.0 gather_fusion.19
  124.4 1.0 gather_fusion.18
  125.4 1.0 gather_fusion.17
  126.5 1.0 gather_fusion.16
  127.5 1.0 gather_fusion.15
  128.6 1.0 gather_fusion.14
  129.6 1.0 gather_fusion.13
  130.7 1.0 gather_fusion.12
  131.7 1.6 %add_subtract_fusion = f32[512,128]{1,0:T(8,128)} fusion(f32[512,128]{1,0:T(8,128)S(1)} %add_subtract_fusion.1, f32[512,128]{1,0:T(8,128)S(1)} %gather_fusion.19, f32[512,128]{1,0:T(8,128)S(1)} %gather_fusion.18, f32[512,128]{1,0:T(8,128)S(1)} %gather_fusion.17, f32[512,128]{1,0:T(8,128)S(1)} %gather_fusion.16, f32[512,128]{1,0:T(8,128)S(1)} %gather_fusion.15, ...), kind=kLoop, calls=%fused_computation.43 | loop fusion | flops 1179648 | bytes 2902016 | tf_op jit(solution)/shard_map/sub | solution.py:122
  (67 shorter events, 2.2 us)
Async XLA Ops:
  0.6 20.2 %copy-start.5 = (s32[1,4]{1,0:T(1,128)S(1)}, s32[1,4]{1,0:T(1,128)}, u32[]{:S(2)}) copy-start(s32[1,4]{1,0:T(1,128)} %param.15) | copy-start | bytes 52
  0.6 20.2 %copy-start.4 = (f32[1,4,128]{2,1,0:T(4,128)S(1)}, f32[1,4,128]{2,1,0:T(4,128)}, u32[]{:S(2)}) copy-start(f32[1,4,128]{2,1,0:T(4,128)} %param.17) | copy-start | bytes 6148
  0.7 20.3 %copy-start.2 = (f32[512]{0:T(512)S(1)}, f32[512]{0:T(512)}, u32[]{:S(2)}) copy-start(f32[512]{0:T(512)} %param.16) | copy-start | bytes 6148
  4.3 20.8 %collective-permute-start = (bf16[1,128,128]{2,1,0:T(8,128)(2,1)S(1)}, bf16[1,128,128]{2,1,0:T(8,128)(2,1)S(1)}, u32[]{:S(2)}, u32[]{:S(2)}) collective-permute-start(bf16[1,128,128]{2,1,0:T(8,128)(2,1)S(1)} %get-tuple-element.24), channel_id=1, source_target_pairs={{0,8},{8,16},{16,24},{1,9},{9,17},{17,25},{2,10},{10,18},{18,26},{... | collective-permute-start | bytes 98312 | tf_op jit(solution)/shard_map/ppermute | solution.py:18
  8.3 16.7 %collective-permute-start.3 = (bf16[1,128,128]{2,1,0:T(8,128)(2,1)S(1)}, bf16[1,128,128]{2,1,0:T(8,128)(2,1)S(1)}, u32[]{:S(2)}, u32[]{:S(2)}) collective-permute-start(bf16[1,128,128]{2,1,0:T(8,128)(2,1)S(1)} %get-tuple-element.25), channel_id=1, source_target_pairs={{1,0},{2,1},{3,2},{4,3},{5,4},{6,5},{7,6},{9,8},{10,9},{11,10},{12... | collective-permute-start | bytes 98312 | tf_op jit(solution)/shard_map/ppermute | solution.py:21
  11.2 13.9 %collective-permute-start.2 = (bf16[1,128,128]{2,1,0:T(8,128)(2,1)S(1)}, bf16[1,128,128]{2,1,0:T(8,128)(2,1)S(1)}, u32[]{:S(2)}, u32[]{:S(2)}) collective-permute-start(bf16[1,128,128]{2,1,0:T(8,128)(2,1)S(1)} %get-tuple-element.26), channel_id=1, source_target_pairs={{0,1},{1,2},{2,3},{3,4},{4,5},{5,6},{6,7},{8,9},{9,10},{10,11},{11... | collective-permute-start | bytes 98312 | tf_op jit(solution)/shard_map/ppermute | solution.py:18
  14.2 10.9 %collective-permute-start.1 = (bf16[1,128,128]{2,1,0:T(8,128)(2,1)S(1)}, bf16[1,128,128]{2,1,0:T(8,128)(2,1)S(1)}, u32[]{:S(2)}, u32[]{:S(2)}) collective-permute-start(bf16[1,128,128]{2,1,0:T(8,128)(2,1)S(1)} %get-tuple-element.27), channel_id=1, source_target_pairs={{8,0},{16,8},{24,16},{9,1},{17,9},{25,17},{10,2},{18,10},{26,18},{... | collective-permute-start | bytes 98312 | tf_op jit(solution)/shard_map/ppermute | solution.py:21
  21.0 4.2 %copy-start.1 = (bf16[1,1024,1024]{2,1,0:T(8,128)(2,1)S(1)}, bf16[1,1024,1024]{2,1,0:T(8,128)(2,1)}, u32[]{:S(2)}) copy-start(bf16[1,1024,1024]{2,1,0:T(8,128)(2,1)} %param.13) | copy-start | bytes 6291460
  25.6 11.0 %collective-permute-start.4 = (f32[1,128,128]{2,1,0:T(8,128)S(1)}, f32[1,128,128]{2,1,0:T(8,128)S(1)}, u32[]{:S(2)}, u32[]{:S(2)}) collective-permute-start(f32[1,128,128]{2,1,0:T(8,128)S(1)} %get-tuple-element.8), channel_id=1, source_target_pairs={{0,8},{8,16},{16,24},{1,9},{9,17},{17,25},{2,10},{10,18},{18,26},{... | collective-permute-start | bytes 196616 | tf_op jit(solution)/shard_map/ppermute | solution.py:18
  29.6 7.0 %collective-permute-start.7 = (f32[1,128,128]{2,1,0:T(8,128)S(1)}, f32[1,128,128]{2,1,0:T(8,128)S(1)}, u32[]{:S(2)}, u32[]{:S(2)}) collective-permute-start(f32[1,128,128]{2,1,0:T(8,128)S(1)} %get-tuple-element.9), channel_id=1, source_target_pairs={{1,0},{2,1},{3,2},{4,3},{5,4},{6,5},{7,6},{9,8},{10,9},{11,10},{12... | collective-permute-start | bytes 196616 | tf_op jit(solution)/shard_map/ppermute | solution.py:21
  31.5 5.1 %collective-permute-start.6 = (f32[1,128,128]{2,1,0:T(8,128)S(1)}, f32[1,128,128]{2,1,0:T(8,128)S(1)}, u32[]{:S(2)}, u32[]{:S(2)}) collective-permute-start(f32[1,128,128]{2,1,0:T(8,128)S(1)} %get-tuple-element.10), channel_id=1, source_target_pairs={{0,1},{1,2},{2,3},{3,4},{4,5},{5,6},{6,7},{8,9},{9,10},{10,11},{11... | collective-permute-start | bytes 196616 | tf_op jit(solution)/shard_map/ppermute | solution.py:18
  35.2 5.0 %collective-permute-start.5 = (f32[1,128,128]{2,1,0:T(8,128)S(1)}, f32[1,128,128]{2,1,0:T(8,128)S(1)}, u32[]{:S(2)}, u32[]{:S(2)}) collective-permute-start(f32[1,128,128]{2,1,0:T(8,128)S(1)} %get-tuple-element.11), channel_id=1, source_target_pairs={{8,0},{16,8},{24,16},{9,1},{17,9},{25,17},{10,2},{18,10},{26,18},{... | collective-permute-start | bytes 196616 | tf_op jit(solution)/shard_map/ppermute | solution.py:21
  45.1 10.3 %collective-permute-start.8 = (f32[1,128,128]{2,1,0:T(8,128)S(1)}, f32[1,128,128]{2,1,0:T(8,128)S(1)}, u32[]{:S(2)}, u32[]{:S(2)}) collective-permute-start(f32[1,128,128]{2,1,0:T(8,128)S(1)} %get-tuple-element.16), channel_id=1, source_target_pairs={{0,8},{8,16},{16,24},{1,9},{9,17},{17,25},{2,10},{10,18},{18,26},{... | collective-permute-start | bytes 196616 | tf_op jit(solution)/shard_map/ppermute | solution.py:18
  48.3 7.1 %collective-permute-start.11 = (f32[1,128,128]{2,1,0:T(8,128)S(1)}, f32[1,128,128]{2,1,0:T(8,128)S(1)}, u32[]{:S(2)}, u32[]{:S(2)}) collective-permute-start(f32[1,128,128]{2,1,0:T(8,128)S(1)} %get-tuple-element.17), channel_id=1, source_target_pairs={{1,0},{2,1},{3,2},{4,3},{5,4},{6,5},{7,6},{9,8},{10,9},{11,10},{12... | collective-permute-start | bytes 196616 | tf_op jit(solution)/shard_map/ppermute | solution.py:21
  50.5 4.9 %collective-permute-start.10 = (f32[1,128,128]{2,1,0:T(8,128)S(1)}, f32[1,128,128]{2,1,0:T(8,128)S(1)}, u32[]{:S(2)}, u32[]{:S(2)}) collective-permute-start(f32[1,128,128]{2,1,0:T(8,128)S(1)} %get-tuple-element.18), channel_id=1, source_target_pairs={{0,1},{1,2},{2,3},{3,4},{4,5},{5,6},{6,7},{8,9},{9,10},{10,11},{11... | collective-permute-start | bytes 196616 | tf_op jit(solution)/shard_map/ppermute | solution.py:18
  54.1 5.0 %collective-permute-start.9 = (f32[1,128,128]{2,1,0:T(8,128)S(1)}, f32[1,128,128]{2,1,0:T(8,128)S(1)}, u32[]{:S(2)}, u32[]{:S(2)}) collective-permute-start(f32[1,128,128]{2,1,0:T(8,128)S(1)} %get-tuple-element.19), channel_id=1, source_target_pairs={{8,0},{16,8},{24,16},{9,1},{17,9},{25,17},{10,2},{18,10},{26,18},{... | collective-permute-start | bytes 196616 | tf_op jit(solution)/shard_map/ppermute | solution.py:21
  69.0 3.3 %copy-start = (f32[512,128]{1,0:T(8,128)S(1)}, f32[512,128]{1,0:T(8,128)}, u32[]{:S(2)}) copy-start(f32[512,128]{1,0:T(8,128)} %param.9) | copy-start | bytes 786436
  75.8 11.4 %collective-permute-start.12 = (bf16[1,128,128]{2,1,0:T(8,128)(2,1)S(1)}, bf16[1,128,128]{2,1,0:T(8,128)(2,1)S(1)}, u32[]{:S(2)}, u32[]{:S(2)}) collective-permute-start(bf16[1,128,128]{2,1,0:T(8,128)(2,1)S(1)} %get-tuple-element.20), channel_id=1, source_target_pairs={{0,8},{8,16},{16,24},{1,9},{9,17},{17,25},{2,10},{10,18},{18,26},{... | collective-permute-start | bytes 98312 | tf_op jit(solution)/shard_map/ppermute | solution.py:18
  79.0 8.2 %collective-permute-start.15 = (bf16[1,128,128]{2,1,0:T(8,128)(2,1)S(1)}, bf16[1,128,128]{2,1,0:T(8,128)(2,1)S(1)}, u32[]{:S(2)}, u32[]{:S(2)}) collective-permute-start(bf16[1,128,128]{2,1,0:T(8,128)(2,1)S(1)} %get-tuple-element.21), channel_id=1, source_target_pairs={{1,0},{2,1},{3,2},{4,3},{5,4},{6,5},{7,6},{9,8},{10,9},{11,10},{12... | collective-permute-start | bytes 98312 | tf_op jit(solution)/shard_map/ppermute | solution.py:21
  81.1 6.1 %collective-permute-start.14 = (bf16[1,128,128]{2,1,0:T(8,128)(2,1)S(1)}, bf16[1,128,128]{2,1,0:T(8,128)(2,1)S(1)}, u32[]{:S(2)}, u32[]{:S(2)}) collective-permute-start(bf16[1,128,128]{2,1,0:T(8,128)(2,1)S(1)} %get-tuple-element.22), channel_id=1, source_target_pairs={{0,1},{1,2},{2,3},{3,4},{4,5},{5,6},{6,7},{8,9},{9,10},{10,11},{11... | collective-permute-start | bytes 98312 | tf_op jit(solution)/shard_map/ppermute | solution.py:18
  85.5 4.7 %collective-permute-start.13 = (bf16[1,128,128]{2,1,0:T(8,128)(2,1)S(1)}, bf16[1,128,128]{2,1,0:T(8,128)(2,1)S(1)}, u32[]{:S(2)}, u32[]{:S(2)}) collective-permute-start(bf16[1,128,128]{2,1,0:T(8,128)(2,1)S(1)} %get-tuple-element.23), channel_id=1, source_target_pairs={{8,0},{16,8},{24,16},{9,1},{17,9},{25,17},{10,2},{18,10},{26,18},{... | collective-permute-start | bytes 98312 | tf_op jit(solution)/shard_map/ppermute | solution.py:21
  90.6 9.8 %collective-permute-start.16 = (f32[1,128,128]{2,1,0:T(8,128)S(1)}, f32[1,128,128]{2,1,0:T(8,128)S(1)}, u32[]{:S(2)}, u32[]{:S(2)}) collective-permute-start(f32[1,128,128]{2,1,0:T(8,128)S(1)} %get-tuple-element.4), channel_id=1, source_target_pairs={{0,8},{8,16},{16,24},{1,9},{9,17},{17,25},{2,10},{10,18},{18,26},{... | collective-permute-start | bytes 196616 | tf_op jit(solution)/shard_map/ppermute | solution.py:18
  92.5 7.9 %collective-permute-start.19 = (f32[1,128,128]{2,1,0:T(8,128)S(1)}, f32[1,128,128]{2,1,0:T(8,128)S(1)}, u32[]{:S(2)}, u32[]{:S(2)}) collective-permute-start(f32[1,128,128]{2,1,0:T(8,128)S(1)} %get-tuple-element.5), channel_id=1, source_target_pairs={{1,0},{2,1},{3,2},{4,3},{5,4},{6,5},{7,6},{9,8},{10,9},{11,10},{12... | collective-permute-start | bytes 196616 | tf_op jit(solution)/shard_map/ppermute | solution.py:21
  94.5 6.0 %collective-permute-start.18 = (f32[1,128,128]{2,1,0:T(8,128)S(1)}, f32[1,128,128]{2,1,0:T(8,128)S(1)}, u32[]{:S(2)}, u32[]{:S(2)}) collective-permute-start(f32[1,128,128]{2,1,0:T(8,128)S(1)} %get-tuple-element.6), channel_id=1, source_target_pairs={{0,1},{1,2},{2,3},{3,4},{4,5},{5,6},{6,7},{8,9},{9,10},{10,11},{11... | collective-permute-start | bytes 196616 | tf_op jit(solution)/shard_map/ppermute | solution.py:18
  99.0 5.0 %collective-permute-start.17 = (f32[1,128,128]{2,1,0:T(8,128)S(1)}, f32[1,128,128]{2,1,0:T(8,128)S(1)}, u32[]{:S(2)}, u32[]{:S(2)}) collective-permute-start(f32[1,128,128]{2,1,0:T(8,128)S(1)} %get-tuple-element.7), channel_id=1, source_target_pairs={{8,0},{16,8},{24,16},{9,1},{17,9},{25,17},{10,2},{18,10},{26,18},{... | collective-permute-start | bytes 196616 | tf_op jit(solution)/shard_map/ppermute | solution.py:21
  109.8 9.7 %collective-permute-start.20 = (f32[1,128,128]{2,1,0:T(8,128)S(1)}, f32[1,128,128]{2,1,0:T(8,128)S(1)}, u32[]{:S(2)}, u32[]{:S(2)}) collective-permute-start(f32[1,128,128]{2,1,0:T(8,128)S(1)} %get-tuple-element.12), channel_id=1, source_target_pairs={{0,8},{8,16},{16,24},{1,9},{9,17},{17,25},{2,10},{10,18},{18,26},{... | collective-permute-start | bytes 196616 | tf_op jit(solution)/shard_map/ppermute | solution.py:18
  111.8 7.8 %collective-permute-start.23 = (f32[1,128,128]{2,1,0:T(8,128)S(1)}, f32[1,128,128]{2,1,0:T(8,128)S(1)}, u32[]{:S(2)}, u32[]{:S(2)}) collective-permute-start(f32[1,128,128]{2,1,0:T(8,128)S(1)} %get-tuple-element.13), channel_id=1, source_target_pairs={{1,0},{2,1},{3,2},{4,3},{5,4},{6,5},{7,6},{9,8},{10,9},{11,10},{12... | collective-permute-start | bytes 196616 | tf_op jit(solution)/shard_map/ppermute | solution.py:21
  113.7 5.9 %collective-permute-start.22 = (f32[1,128,128]{2,1,0:T(8,128)S(1)}, f32[1,128,128]{2,1,0:T(8,128)S(1)}, u32[]{:S(2)}, u32[]{:S(2)}) collective-permute-start(f32[1,128,128]{2,1,0:T(8,128)S(1)} %get-tuple-element.14), channel_id=1, source_target_pairs={{0,1},{1,2},{2,3},{3,4},{4,5},{5,6},{6,7},{8,9},{9,10},{10,11},{11... | collective-permute-start | bytes 196616 | tf_op jit(solution)/shard_map/ppermute | solution.py:18
  118.3 5.0 %collective-permute-start.21 = (f32[1,128,128]{2,1,0:T(8,128)S(1)}, f32[1,128,128]{2,1,0:T(8,128)S(1)}, u32[]{:S(2)}, u32[]{:S(2)}) collective-permute-start(f32[1,128,128]{2,1,0:T(8,128)S(1)} %get-tuple-element.15), channel_id=1, source_target_pairs={{8,0},{16,8},{24,16},{9,1},{17,9},{25,17},{10,2},{18,10},{26,18},{... | collective-permute-start | bytes 196616 | tf_op jit(solution)/shard_map/ppermute | solution.py:21
  129.6 2.1 %copy-start.3 = (f32[512]{0:T(512)S(1)}, f32[512]{0:T(512)}, u32[]{:S(2)}) copy-start(f32[512]{0:T(512)} %param.10) | copy-start | bytes 6148
where the time goes:
time: 136 us; the launch traced here: 133 us
  starting transfers between devices  62.5 us (46%)
  local copies, waits for them, and re-layouts  27.7 us (20%)
  other arithmetic  21.2 us (16%)
  waiting for transfers between devices  17.4 us (13%)
  matrix products  3.01 us (2%)
  between operations  1.44 us (1%)
    ppermute x12, starting transfers between devices, with_halo(): lax.ppermute(lax.slice_in_dim(block, block.shape[dim] - width, None, axis...  41.9 us
    gather x16, local copies, waits for them, and re-layouts, precision_apply(): extended[prec_columns[entry]]  21.4 us
    ppermute x12, starting transfers between devices, with_halo(): lax.ppermute(lax.slice_in_dim(block, 0, width, axis=dim), axis, backward)  20.6 us
    ppermute x12, waiting for transfers between devices, with_halo(): lax.ppermute(lax.slice_in_dim(block, 0, width, axis=dim), axis, backward)  17.3 us
    scatter-add x2, other arithmetic, precondition(): numerator.at[flat_list]  7.01 us
    gather x4, local copies, waits for them, and re-layouts, pack_rows(): return jnp.where(filled[:, :, None], vector[send_list[0]], 0.0)  5.13 us
    scatter-add x1, other arithmetic, precondition(): denominator = own_weight.at[flat_list].add(slot_weight.reshape(-1))  4.09 us
    sub x2, other arithmetic, per_device(): residual - precision_apply(direction, ghosts, prec_diag, prec_values, pre...  3.78 us
  transfers between devices with their start and end apart: 24, of which 5 were waited for; matrix products, arithmetic and copies ran while one was open for 8% of the time, Pallas kernels for 0%

commit v1 on v0

v1 whole, which is shorter than its diff:
```python
import functools

import jax
import jax.numpy as jnp
from jax import lax
from jax.experimental import pallas as pl
from jax.experimental.pallas import tpu as pltpu
from jax.sharding import PartitionSpec as P

ITERS = 2
LOWER = 0.25
UPPER = 2.0

MESH = pl.DeviceIdType.MESH
LANES = 128
F32 = jnp.float32
BF16 = jnp.bfloat16


def dot_nn(left, right):
    return lax.dot_general(left, right, (((1,), (0,)), ((), ())), preferred_element_type=F32)


def dot_nt(left, right):
    return lax.dot_general(left, right, (((1,), (1,)), ((), ())), preferred_element_type=F32)


def kernel(
    n_x,
    n_y,
    right_ref,
    diag_ref,
    values_ref,
    columns_ref,
    inverse_hbm,
    list_ref,
    count_ref,
    own_ref,
    copy_ref,
    solution_ref,
    residual_ref,
    inverse,
    pick,
    coupling,
    send,
    recv,
    inverse_sem,
    send_sem,
    recv_sem,
):
    row = lax.axis_index("gx")
    col = lax.axis_index("gy")
    live = (row > 0, row < n_x - 1, col > 0, col < n_y - 1)
    target = ((row - 1, col), (row + 1, col), (row, col - 1), (row, col + 1))
    own = right_ref.shape[0]
    slots = list_ref.shape[2]
    entries = values_ref.shape[0]
    total = inverse.shape[0]
    rounds = recv.shape[0]

    load = pltpu.make_async_copy(inverse_hbm.at[0], inverse, inverse_sem)
    load.start()

    barrier = pltpu.get_barrier_semaphore()
    for k in range(4):

        @pl.when(live[k])
        def _():
            pl.semaphore_signal(barrier, inc=1, device_id=target[k], device_id_type=MESH)

    residual = jnp.transpose(right_ref[...])

    slot_id = lax.broadcasted_iota(jnp.int32, (1, slots), 1)
    node_id = lax.broadcasted_iota(jnp.int32, (own, slots), 0)
    weights = []
    for k in range(4):
        filled = slot_id < count_ref[0, k]
        chosen = jnp.where(filled, list_ref[0, k : k + 1, :], -1)
        pick[:, k * slots : (k + 1) * slots] = jnp.where(node_id == chosen, 1.0, 0.0).astype(BF16)
        inside = slot_id < jnp.where(live[k], count_ref[0, k], 0)
        weights.append(jnp.where(inside, copy_ref[0, k : k + 1, :], 0.0))
    weight = jnp.concatenate(weights, axis=1)

    for k in range(4):

        @pl.when(jnp.logical_not(live[k]))
        def _():
            for stage in range(rounds):
                recv[stage, k] = jnp.zeros(recv.shape[2:], recv.dtype)

    def copy(stage, k, peer):
        return pltpu.make_async_remote_copy(
            src_ref=send.at[stage, k],
            dst_ref=recv.at[stage, peer],
            send_sem=send_sem.at[stage, k],
            recv_sem=recv_sem.at[stage, peer],
            device_id=target[k],
            device_id_type=MESH,
        )

    def start(stage, blocks):
        for k in range(4):
            send[stage, k] = blocks[:, k * slots : (k + 1) * slots].astype(BF16)
        for k in range(4):

            @pl.when(live[k])
            def _():
                copy(stage, k, k ^ 1).start()

    def finish(stage):
        for k in range(4):

            @pl.when(live[k])
            def _():
                copy(stage, k, k).wait_recv()

        return jnp.concatenate([recv[stage, k] for k in range(4)], axis=1)

    def build_coupling(first, last):
        step = 16
        base = lax.broadcasted_iota(jnp.int32, (step, LANES), 0)
        for tile in range(own // LANES):
            lanes = slice(tile * LANES, (tile + 1) * LANES)
            columns = [jnp.broadcast_to(columns_ref[j : j + 1, lanes], (step, LANES)) for j in range(entries)]
            values = [jnp.broadcast_to(values_ref[j : j + 1, lanes], (step, LANES)) for j in range(entries)]

            def body(m, carry):
                here = base + m * step
                parts = [jnp.where(columns[j] == here, values[j], 0.0) for j in range(entries)]
                while len(parts) > 1:
                    parts = [sum(parts[i : i + 2][1:], parts[i]) for i in range(0, len(parts), 2)]
                coupling[pl.ds(pl.multiple_of(m * step, step), step), lanes] = parts[0].astype(BF16)
                return carry

            lax.fori_loop(first // step, last // step, body, 0, unroll=4)

    center = 0.5 * (UPPER + LOWER)
    spread = 0.5 * (UPPER - LOWER)
    sigma = center / spread
    diag = diag_ref[...]
    own_weight = own_ref[...]

    picked = dot_nn(residual.astype(BF16), pick[...])

    pl.semaphore_wait(barrier, sum(jnp.where(here, 1, 0) for here in live))

    ratio = 1.0 / sigma
    direction = None
    solution = None
    stage = 0
    inverse_denominator = None
    for iteration in range(ITERS):
        start(stage, picked)
        half = residual.astype(BF16)
        if iteration == 0:
            high = weight.astype(BF16)
            rest = weight - high.astype(F32)
            middle = rest.astype(BF16)
            low = (rest - middle.astype(F32)).astype(BF16)
            pieces = jnp.concatenate([jnp.broadcast_to(x, (16, 4 * slots)) for x in (high, middle, low)], axis=0)
            spread_weight = dot_nt(pieces, pick[...])
            denominator = own_weight + (spread_weight[0:1] + spread_weight[16:17] + spread_weight[32:33])
            inverse_denominator = 1.0 / denominator
            build_coupling(0, total // 2)
            load.wait()
        term_ghost = dot_nt(half, inverse[own:, :own])
        term_own = dot_nt(half, inverse[:own, :own])
        ghosts = finish(stage)
        start(stage + 1, term_ghost + dot_nt(ghosts, inverse[own:, own:]))
        term_own = term_own + dot_nt(ghosts, inverse[:own, own:])
        if iteration == 0:
            build_coupling(total // 2, total)
        returned = finish(stage + 1)
        weighted = (weight * returned.astype(F32)).astype(BF16)
        update = (own_weight * term_own + dot_nt(weighted, pick[...])) * inverse_denominator
        if iteration == 0:
            direction = update * (1.0 / center)
        else:
            ratio_next = 1.0 / (2.0 * sigma - ratio)
            direction = (ratio_next * ratio) * direction + (2.0 * ratio_next / spread) * update
            ratio = ratio_next
        half = direction.astype(BF16)
        start(stage + 2, dot_nn(half, pick[...]))
        solution = direction if solution is None else solution + direction
        residual = residual - diag * direction - dot_nn(half, coupling[:own, :])
        if iteration == ITERS - 1:
            solution_ref[...] = jnp.transpose(solution)
        ghosts = finish(stage + 2)
        residual = residual - dot_nn(ghosts, coupling[own:, :])
        if iteration < ITERS - 1:
            picked = dot_nn(residual.astype(BF16), pick[...])
        stage += 3
    residual_ref[...] = jnp.transpose(residual)

    for stage in range(rounds):
        for k in range(4):

            @pl.when(live[k])
            def _():
                copy(stage, k, k ^ 1).wait_send()


def per_device(n_x, n_y, right_side, prec_diag, prec_values, prec_columns, inverse, send_list, send_count, own_weight, copy_weight):
    own, width = right_side.shape
    total = inverse.shape[1]
    slots = send_list.shape[2]
    rounds = 3 * ITERS
    vmem = pl.BlockSpec(memory_space=pltpu.VMEM)
    out = jax.ShapeDtypeStruct((own, width), F32)
    return pl.pallas_call(
        functools.partial(kernel, n_x, n_y),
        out_shape=(out, out),
        in_specs=[
            vmem,
            vmem,
            vmem,
            vmem,
            pl.BlockSpec(memory_space=pl.ANY),
            vmem,
            pl.BlockSpec(memory_space=pltpu.SMEM),
            vmem,
            vmem,
        ],
        out_specs=(vmem, vmem),
        scratch_shapes=[
            pltpu.VMEM((total, total), BF16),
            pltpu.VMEM((own, 4 * slots), BF16),
            pltpu.VMEM((total, own), BF16),
            pltpu.VMEM((rounds, 4, width, slots), BF16),
            pltpu.VMEM((rounds, 4, width, slots), BF16),
            pltpu.SemaphoreType.DMA,
            pltpu.SemaphoreType.DMA((rounds, 4)),
            pltpu.SemaphoreType.DMA((rounds, 4)),
        ],
        compiler_params=pltpu.CompilerParams(collective_id=0, has_side_effects=True),
    )(
        right_side,
        prec_diag.reshape(1, own),
        prec_values,
        prec_columns,
        inverse,
        send_list,
        send_count,
        own_weight.reshape(1, own),
        copy_weight,
    )


def solution(mesh):
    return jax.shard_map(
        functools.partial(per_device, mesh.shape["gx"], mesh.shape["gy"]),
        mesh=mesh,
        in_specs=(
            P(("gx", "gy"), None),
            P(("gx", "gy")),
            P(None, ("gx", "gy")),
            P(None, ("gx", "gy")),
            P(("gx", "gy"), None, None),
            P(("gx", "gy"), None, None),
            P(("gx", "gy"), None),
            P(("gx", "gy")),
            P(("gx", "gy"), None, None),
        ),
        out_specs=(P(("gx", "gy"), None), P(("gx", "gy"), None)),
        check_vma=False,
    )
```

time: 136 us -> 31 us (0.23); the launches traced: 133 us -> 30.6 us
  starting transfers between devices: 62.5 us -> 0 us
  Pallas kernels: 0 us -> 26.7 us
  local copies, waits for them, and re-layouts: 27.7 us -> 3.34 us
  other arithmetic: 21.2 us -> 0 us
  waiting for transfers between devices: 17.4 us -> 0 us
  matrix products: 3.01 us -> 0 us
    ppermute x24 -> x0, starting transfers between devices: 62.5 us -> none  [the longest x12 41.9 us: with_halo(): lax.ppermute(lax.slice_in_dim(block, block.shape[dim] - width, None, axis...]
    pallas_call x0 -> x1, Pallas kernels: none -> 26.7 us  [per_device(): pl.pallas_call(functools.partial(kernel, n_x, n_y), out_shape=(out, out),...]
    gather x20 -> x0, local copies, waits for them, and re-layouts: 26.6 us -> none  [the longest x16 21.4 us: precision_apply(): extended[prec_columns[entry]]]
    ppermute x24 -> x0, waiting for transfers between devices: 17.4 us -> none  [the longest x12 17.3 us: with_halo(): lax.ppermute(lax.slice_in_dim(block, 0, width, axis=dim), axis, backward)]
    scatter-add x3 -> x0, other arithmetic: 11.1 us -> none  [the longest x2 7.01 us: precondition(): numerator.at[flat_list]]
    sub x2 -> x0, other arithmetic: 3.78 us -> none  [per_device(): residual - precision_apply(direction, ghosts, prec_diag, prec_values, pre...]
    unnamed x13 -> x2, local copies, waits for them, and re-layouts: 0.03 us -> 3.34 us
    dot_general x4 -> x0, matrix products: 3.01 us -> none  [the longest x2 2.14 us: precondition(): jnp.dot(matrix[:, :owned_rows], owned_half, preferred_element_type=jnp.fl...]
  transfers between devices with their start and end apart: 24 -> 0, of which waited for: 5 -> 0; matrix products, arithmetic and copies ran while one was open for 8% -> 0% of each run, Pallas kernels for 0% -> 0%
where the time goes in v1:
time: 31 us; the launch traced here: 30.6 us
  Pallas kernels  26.7 us (86%)
  local copies, waits for them, and re-layouts  3.34 us (11%)
  between operations  0.64 us (2%)
    pallas_call x1, Pallas kernels, per_device(): pl.pallas_call(functools.partial(kernel, n_x, n_y), out_shape=(out, out),...  26.7 us
    unnamed x2, local copies, waits for them, and re-layouts  3.34 us

profile of v1, /device:TPU:1, one launch (start us, length us, event | category | flops | bytes accessed | tf_op | source)
XLA Modules:
  0.0 30.6 jit_solution(5664853443010328954)
XLA Ops:
  0.6 26.7 %shard_map.104 = (f32[512,128]{1,0:T(8,128)}, f32[512,128]{1,0:T(8,128)}) custom-call(f32[512,128]{1,0:T(8,128)} %right_ref.1, f32[1,512]{1,0:T(1,128)} %bitcast.2, f32[8,512]{1,0:T(8,128)} %values_ref.1, s32[8,512]{1,0:T(8,128)} %columns_ref.1, bf16[1,1024,1024]{2,1,0:T(8,128)(2,1)} %inverse_hbm.1, s32[1,4,128]{2,1,0:T(4,128)} %list_ref.1, ...), custom_call_target="tpu_custom_call" | custom-call | tf_op jit(solution)/shard_map/pallas_call | solution.py:210
  27.3 1.7 %copy.13 = f32[512,128]{1,0:T(8,128)} copy(f32[512,128]{1,0:T(8,128)} %get-tuple-element.4) | data formatting | bytes 524288
  29.0 1.7 %copy.14 = f32[512,128]{1,0:T(8,128)} copy(f32[512,128]{1,0:T(8,128)} %get-tuple-element.5) | data formatting | bytes 524288

commit v2 on v1

--- a/solution.py
+++ b/solution.py
@@ -28,23 +28,30 @@
 def kernel(
     n_x,
     n_y,
+    right_hbm,
+    diag_hbm,
+    values_hbm,
+    columns_hbm,
+    inverse_hbm,
+    list_hbm,
+    count_ref,
+    own_hbm,
+    copy_hbm,
+    solution_ref,
+    residual_ref,
     right_ref,
     diag_ref,
     values_ref,
     columns_ref,
-    inverse_hbm,
     list_ref,
-    count_ref,
     own_ref,
     copy_ref,
-    solution_ref,
-    residual_ref,
     inverse,
     pick,
     coupling,
     send,
     recv,
-    inverse_sem,
+    load_sem,
     send_sem,
     recv_sem,
 ):
@@ -53,14 +60,11 @@
     live = (row > 0, row < n_x - 1, col > 0, col < n_y - 1)
     target = ((row - 1, col), (row + 1, col), (row, col - 1), (row, col + 1))
     own = right_ref.shape[0]
-    slots = list_ref.shape[2]
+    slots = list_ref.shape[1]
     entries = values_ref.shape[0]
     total = inverse.shape[0]
     rounds = recv.shape[0]
 
-    load = pltpu.make_async_copy(inverse_hbm.at[0], inverse, inverse_sem)
-    load.start()
-
     barrier = pltpu.get_barrier_semaphore()
     for k in range(4):
 
@@ -68,18 +72,33 @@
         def _():
             pl.semaphore_signal(barrier, inc=1, device_id=target[k], device_id_type=MESH)
 
-    residual = jnp.transpose(right_ref[...])
-
+    loads = [
+        pltpu.make_async_copy(source, place, load_sem.at[i])
+        for i, (source, place) in enumerate(
+            (
+                (list_hbm.at[0], list_ref),
+                (right_hbm, right_ref),
+                (copy_hbm.at[0], copy_ref),
+                (columns_hbm, columns_ref),
+                (values_hbm, values_ref),
+                (own_hbm, own_ref),
+                (diag_hbm, diag_ref),
+                (inverse_hbm.at[0], inverse),
+            )
+        )
+    ]
+    for load in loads:
+        load.start()
+    loads[0].wait()
     slot_id = lax.broadcasted_iota(jnp.int32, (1, slots), 1)
     node_id = lax.broadcasted_iota(jnp.int32, (own, slots), 0)
-    weights = []
     for k in range(4):
         filled = slot_id < count_ref[0, k]
-        chosen = jnp.where(filled, list_ref[0, k : k + 1, :], -1)
+        chosen = jnp.where(filled, list_ref[k : k + 1, :], -1)
         pick[:, k * slots : (k + 1) * slots] = jnp.where(node_id == chosen, 1.0, 0.0).astype(BF16)
-        inside = slot_id < jnp.where(live[k], count_ref[0, k], 0)
-        weights.append(jnp.where(inside, copy_ref[0, k : k + 1, :], 0.0))
-    weight = jnp.concatenate(weights, axis=1)
+
+    loads[1].wait()
+    residual = jnp.transpose(right_ref[...])
 
     for k in range(4):
 
@@ -137,9 +156,6 @@
     center = 0.5 * (UPPER + LOWER)
     spread = 0.5 * (UPPER - LOWER)
     sigma = center / spread
-    diag = diag_ref[...]
-    own_weight = own_ref[...]
-
     picked = dot_nn(residual.astype(BF16), pick[...])
 
     pl.semaphore_wait(barrier, sum(jnp.where(here, 1, 0) for here in live))
@@ -153,6 +169,15 @@
         start(stage, picked)
         half = residual.astype(BF16)
         if iteration == 0:
+            for load in loads[2:7]:
+                load.wait()
+            diag = diag_ref[...]
+            own_weight = own_ref[...]
+            weights = []
+            for k in range(4):
+                inside = slot_id < jnp.where(live[k], count_ref[0, k], 0)
+                weights.append(jnp.where(inside, copy_ref[k : k + 1, :], 0.0))
+            weight = jnp.concatenate(weights, axis=1)
             high = weight.astype(BF16)
             rest = weight - high.astype(F32)
             middle = rest.astype(BF16)
@@ -162,7 +187,7 @@
             denominator = own_weight + (spread_weight[0:1] + spread_weight[16:17] + spread_weight[32:33])
             inverse_denominator = 1.0 / denominator
             build_coupling(0, total // 2)
-            load.wait()
+            loads[7].wait()
         term_ghost = dot_nt(half, inverse[own:, :own])
         term_own = dot_nt(half, inverse[:own, :own])
         ghosts = finish(stage)
@@ -184,13 +209,13 @@
         solution = direction if solution is None else solution + direction
         residual = residual - diag * direction - dot_nn(half, coupling[:own, :])
         if iteration == ITERS - 1:
-            solution_ref[...] = jnp.transpose(solution)
+            solution_ref[...] = solution
         ghosts = finish(stage + 2)
         residual = residual - dot_nn(ghosts, coupling[own:, :])
         if iteration < ITERS - 1:
             picked = dot_nn(residual.astype(BF16), pick[...])
         stage += 3
-    residual_ref[...] = jnp.transpose(residual)
+    residual_ref[...] = residual
 
     for stage in range(rounds):
         for k in range(4):
@@ -198,6 +223,11 @@
             @pl.when(live[k])
             def _():
                 copy(stage, k, k ^ 1).wait_send()
+
+
+def flip(solution_in, residual_in, solution_ref, residual_ref):
+    solution_ref[...] = jnp.transpose(solution_in[...])
+    residual_ref[...] = jnp.transpose(residual_in[...])
 
 
 def per_device(n_x, n_y, right_side, prec_diag, prec_values, prec_columns, inverse, send_list, send_count, own_weight, copy_weight):
@@ -206,33 +236,32 @@
     slots = send_list.shape[2]
     rounds = 3 * ITERS
     vmem = pl.BlockSpec(memory_space=pltpu.VMEM)
+    hbm = pl.BlockSpec(memory_space=pltpu.HBM)
+    field = pltpu.VMEM((width, own), F32)
     out = jax.ShapeDtypeStruct((own, width), F32)
-    return pl.pallas_call(
+    flipped = pl.pallas_call(
         functools.partial(kernel, n_x, n_y),
-        out_shape=(out, out),
-        in_specs=[
-            vmem,
-            vmem,
-            vmem,
-            vmem,
-            pl.BlockSpec(memory_space=pl.ANY),
-            vmem,
-            pl.BlockSpec(memory_space=pltpu.SMEM),
-            vmem,
-            vmem,
-        ],
+        out_shape=(field, field),
+        in_specs=[hbm] * 6 + [pl.BlockSpec(memory_space=pltpu.SMEM)] + [hbm] * 2,
         out_specs=(vmem, vmem),
         scratch_shapes=[
+            pltpu.VMEM(right_side.shape, F32),
+            pltpu.VMEM((1, own), F32),
+            pltpu.VMEM(prec_values.shape, F32),
+            pltpu.VMEM(prec_columns.shape, jnp.int32),
+            pltpu.VMEM((4, slots), jnp.int32),
+            pltpu.VMEM((1, own), F32),
+            pltpu.VMEM((4, slots), F32),
             pltpu.VMEM((total, total), BF16),
             pltpu.VMEM((own, 4 * slots), BF16),
             pltpu.VMEM((total, own), BF16),
             pltpu.VMEM((rounds, 4, width, slots), BF16),
             pltpu.VMEM((rounds, 4, width, slots), BF16),
-            pltpu.SemaphoreType.DMA,
+            pltpu.SemaphoreType.DMA((8,)),
             pltpu.SemaphoreType.DMA((rounds, 4)),
             pltpu.SemaphoreType.DMA((rounds, 4)),
         ],
-        compiler_params=pltpu.CompilerParams(collective_id=0, has_side_effects=True),
+        compiler_params=pltpu.CompilerParams(collective_id=0, has_side_effects=True, vmem_limit_bytes=62 * 2**20 + 2**19),
     )(
         right_side,
         prec_diag.reshape(1, own),
@@ -244,6 +273,13 @@
         own_weight.reshape(1, own),
         copy_weight,
     )
+    return pl.pallas_call(
+        flip,
+        out_shape=(out, out),
+        in_specs=[vmem, vmem],
+        out_specs=(vmem, vmem),
+        compiler_params=pltpu.CompilerParams(vmem_limit_bytes=16 * 2**20),
+    )(*flipped)
 
 
 def solution(mesh):

time: 31 us -> 27.5 us (0.89)
  local copies, waits for them, and re-layouts: 3.34 us -> 0 us
    unnamed x2 -> x0, local copies, waits for them, and re-layouts: 3.34 us -> none
    pallas_call x1 -> x2, Pallas kernels: 26.7 us -> 26.5 us  [the longest x1 25.6 us: per_device(): pl.pallas_call(functools.partial(kernel, n_x, n_y), out_shape=(field, fie...]
where the time goes in v2:
time: 27.5 us; the launch traced here: 27.2 us
  Pallas kernels  26.5 us (96%)
  between operations  0.64 us (2%)
    pallas_call x1, Pallas kernels, per_device(): pl.pallas_call(functools.partial(kernel, n_x, n_y), out_shape=(field, fie...  25.6 us
    pallas_call x1, Pallas kernels, per_device(): pl.pallas_call(flip, out_shape=(out, out), in_specs=[vmem, vmem], out_spe...  0.92 us

profile of v2, /device:TPU:1, one launch (start us, length us, event | category | flops | bytes accessed | tf_op | source)
XLA Modules:
  0.0 27.2 jit_solution(7274126108303073108)
XLA Ops:
  0.6 25.6 %shard_map.104 = (f32[128,512]{1,0:T(8,128)S(1)}, f32[128,512]{1,0:T(8,128)S(1)}) custom-call(f32[512,128]{1,0:T(8,128)} %right_hbm.1, f32[1,512]{1,0:T(1,128)} %bitcast.2, f32[8,512]{1,0:T(8,128)} %values_hbm.1, s32[8,512]{1,0:T(8,128)} %columns_hbm.1, bf16[1,1024,1024]{2,1,0:T(8,128)(2,1)} %inverse_hbm.1, s32[1,4,128]{2,1,0:T(4,128)} %list_hbm.1, ...), custom_call_target="tpu_custom_call" | custom-call | tf_op jit(solution)/shard_map/pallas_call | solution.py:242
  26.2 0.9 %shard_map.105 = (f32[512,128]{1,0:T(8,128)}, f32[512,128]{1,0:T(8,128)}) custom-call(f32[128,512]{1,0:T(8,128)S(1)} %get-tuple-element.4.solution_in, f32[128,512]{1,0:T(8,128)S(1)} %get-tuple-element.5.residual_in), custom_call_target="tpu_custom_call" | custom-call | tf_op jit(solution)/shard_map/pallas_call | solution.py:276

commit v3 on v2

--- a/solution.py
+++ b/solution.py
@@ -15,6 +15,8 @@
 LANES = 128
 F32 = jnp.float32
 BF16 = jnp.bfloat16
+PARTS = 2
+ORDER = (0, 1, 2, 3)
 
 
 def dot_nn(left, right):
@@ -98,42 +100,51 @@
         pick[:, k * slots : (k + 1) * slots] = jnp.where(node_id == chosen, 1.0, 0.0).astype(BF16)
 
     loads[1].wait()
-    residual = jnp.transpose(right_ref[...])
+    field = jnp.transpose(right_ref[...])
+    rows = field.shape[0] // PARTS
+    parts = range(PARTS)
+    residual = [field[part * rows : (part + 1) * rows] for part in parts]
 
     for k in range(4):
 
         @pl.when(jnp.logical_not(live[k]))
         def _():
             for stage in range(rounds):
-                recv[stage, k] = jnp.zeros(recv.shape[2:], recv.dtype)
-
-    def copy(stage, k, peer):
+                for part in range(PARTS):
+                    recv[stage, part, k] = jnp.zeros(recv.shape[3:], recv.dtype)
+
+    def copy(stage, part, k, peer):
+        turn = stage % 2
         return pltpu.make_async_remote_copy(
-            src_ref=send.at[stage, k],
-            dst_ref=recv.at[stage, peer],
-            send_sem=send_sem.at[stage, k],
-            recv_sem=recv_sem.at[stage, peer],
+            src_ref=send.at[stage, part, k],
+            dst_ref=recv.at[stage, part, peer],
+            send_sem=send_sem.at[turn, part, k],
+            recv_sem=recv_sem.at[turn, part, peer],
             device_id=target[k],
             device_id_type=MESH,
         )
 
-    def start(stage, blocks):
-        for k in range(4):
-            send[stage, k] = blocks[:, k * slots : (k + 1) * slots].astype(BF16)
+    def start(stage, part, block):
+        for k in ORDER:
+            send[stage, part, k] = block(slice(k * slots, (k + 1) * slots)).astype(BF16)
+        for k in ORDER:
+            launch(stage, part, k)
+
+    def launch(stage, part, k):
+        @pl.when(live[k])
+        def _():
+            if stage >= 2:
+                copy(stage - 2, part, k, k ^ 1).wait_send()
+            copy(stage, part, k, k ^ 1).start()
+
+    def finish(stage, part):
         for k in range(4):
 
             @pl.when(live[k])
             def _():
-                copy(stage, k, k ^ 1).start()
-
-    def finish(stage):
-        for k in range(4):
-
-            @pl.when(live[k])
-            def _():
-                copy(stage, k, k).wait_recv()
-
-        return jnp.concatenate([recv[stage, k] for k in range(4)], axis=1)
+                copy(stage, part, k, k).wait_recv()
+
+        return jnp.concatenate([recv[stage, part, k] for k in range(4)], axis=1)
 
     def build_coupling(first, last):
         step = 16
@@ -156,18 +167,19 @@
     center = 0.5 * (UPPER + LOWER)
     spread = 0.5 * (UPPER - LOWER)
     sigma = center / spread
-    picked = dot_nn(residual.astype(BF16), pick[...])
+    half = [x.astype(BF16) for x in residual]
+    picked = [dot_nn(x, pick[...]).astype(BF16) for x in half]
 
     pl.semaphore_wait(barrier, sum(jnp.where(here, 1, 0) for here in live))
 
+    for part in parts:
+        start(0, part, lambda lanes: picked[part][:, lanes])
+
     ratio = 1.0 / sigma
-    direction = None
-    solution = None
+    direction = [None] * PARTS
+    solution = [None] * PARTS
     stage = 0
-    inverse_denominator = None
     for iteration in range(ITERS):
-        start(stage, picked)
-        half = residual.astype(BF16)
         if iteration == 0:
             for load in loads[2:7]:
                 load.wait()
@@ -188,41 +200,54 @@
             inverse_denominator = 1.0 / denominator
             build_coupling(0, total // 2)
             loads[7].wait()
-        term_ghost = dot_nt(half, inverse[own:, :own])
-        term_own = dot_nt(half, inverse[:own, :own])
-        ghosts = finish(stage)
-        start(stage + 1, term_ghost + dot_nt(ghosts, inverse[own:, own:]))
-        term_own = term_own + dot_nt(ghosts, inverse[:own, own:])
+        term_ghost = [dot_nt(x, inverse[own:, :own]) for x in half]
+        term_own = [dot_nt(x, inverse[:own, :own]) for x in half]
+        ghosts = [None] * PARTS
+        for part in parts:
+            ghosts[part] = finish(stage, part)
+            whole = term_ghost[part] + dot_nt(ghosts[part], inverse[own:, own:])
+            start(stage + 1, part, lambda lanes: whole[:, lanes])
+        term_own = [own_weight * (term_own[part] + dot_nt(ghosts[part], inverse[:own, own:])) for part in parts]
         if iteration == 0:
             build_coupling(total // 2, total)
-        returned = finish(stage + 1)
-        weighted = (weight * returned.astype(F32)).astype(BF16)
-        update = (own_weight * term_own + dot_nt(weighted, pick[...])) * inverse_denominator
-        if iteration == 0:
-            direction = update * (1.0 / center)
         else:
             ratio_next = 1.0 / (2.0 * sigma - ratio)
-            direction = (ratio_next * ratio) * direction + (2.0 * ratio_next / spread) * update
+        for part in parts:
+            returned = finish(stage + 1, part)
+            weighted = (weight * returned.astype(F32)).astype(BF16)
+            update = (term_own[part] + dot_nt(weighted, pick[...])) * inverse_denominator
+            if iteration == 0:
+                direction[part] = update * (1.0 / center)
+            else:
+                direction[part] = (ratio_next * ratio) * direction[part] + (2.0 * ratio_next / spread) * update
+            half[part] = direction[part].astype(BF16)
+            whole = dot_nn(half[part], pick[...])
+            start(stage + 2, part, lambda lanes: whole[:, lanes])
+        if iteration > 0:
             ratio = ratio_next
-        half = direction.astype(BF16)
-        start(stage + 2, dot_nn(half, pick[...]))
-        solution = direction if solution is None else solution + direction
-        residual = residual - diag * direction - dot_nn(half, coupling[:own, :])
-        if iteration == ITERS - 1:
-            solution_ref[...] = solution
-        ghosts = finish(stage + 2)
-        residual = residual - dot_nn(ghosts, coupling[own:, :])
-        if iteration < ITERS - 1:
-            picked = dot_nn(residual.astype(BF16), pick[...])
+        for part in parts:
+            solution[part] = direction[part] if iteration == 0 else solution[part] + direction[part]
+            residual[part] = residual[part] - diag * direction[part] - dot_nn(half[part], coupling[:own, :])
+            if iteration == ITERS - 1:
+                solution_ref[part * rows : (part + 1) * rows, :] = solution[part]
+        for part in parts:
+            ghosts[part] = finish(stage + 2, part)
+            residual[part] = residual[part] - dot_nn(ghosts[part], coupling[own:, :])
+            if iteration < ITERS - 1:
+                half[part] = residual[part].astype(BF16)
+                whole = dot_nn(half[part], pick[...])
+                start(stage + 3, part, lambda lanes: whole[:, lanes])
+            else:
+                residual_ref[part * rows : (part + 1) * rows, :] = residual[part]
         stage += 3
-    residual_ref[...] = residual
-
-    for stage in range(rounds):
-        for k in range(4):
-
-            @pl.when(live[k])
-            def _():
-                copy(stage, k, k ^ 1).wait_send()
+
+    for stage in range(max(rounds - 2, 0), rounds):
+        for part in parts:
+            for k in range(4):
+
+                @pl.when(live[k])
+                def _():
+                    copy(stage, part, k, k ^ 1).wait_send()
 
 
 def flip(solution_in, residual_in, solution_ref, residual_ref):
@@ -255,11 +280,11 @@
             pltpu.VMEM((total, total), BF16),
             pltpu.VMEM((own, 4 * slots), BF16),
             pltpu.VMEM((total, own), BF16),
-            pltpu.VMEM((rounds, 4, width, slots), BF16),
-            pltpu.VMEM((rounds, 4, width, slots), BF16),
+            pltpu.VMEM((rounds, PARTS, 4, width // PARTS, slots), BF16),
+            pltpu.VMEM((rounds, PARTS, 4, width // PARTS, slots), BF16),
             pltpu.SemaphoreType.DMA((8,)),
-            pltpu.SemaphoreType.DMA((rounds, 4)),
-            pltpu.SemaphoreType.DMA((rounds, 4)),
+            pltpu.SemaphoreType.DMA((2, PARTS, 4)),
+            pltpu.SemaphoreType.DMA((2, PARTS, 4)),
         ],
         compiler_params=pltpu.CompilerParams(collective_id=0, has_side_effects=True, vmem_limit_bytes=62 * 2**20 + 2**19),
     )(

time: 27.5 us -> 26.7 us (0.971)
  Pallas kernels: 26.5 us -> 25.9 us
    pallas_call x1, Pallas kernels: 25.6 us -> 24.9 us  [per_device(): pl.pallas_call(functools.partial(kernel, n_x, n_y), out_shape=(field, fie...]
where the time goes in v3:
time: 26.7 us; the launch traced here: 26.5 us
  Pallas kernels  25.9 us (97%)
  between operations  0.64 us (2%)
    pallas_call x1, Pallas kernels, per_device(): pl.pallas_call(functools.partial(kernel, n_x, n_y), out_shape=(field, fie...  24.9 us
    pallas_call x1, Pallas kernels, per_device(): pl.pallas_call(flip, out_shape=(out, out), in_specs=[vmem, vmem], out_spe...  0.92 us

profile of v3, /device:TPU:1, one launch (start us, length us, event | category | flops | bytes accessed | tf_op | source)
XLA Modules:
  0.0 26.5 jit_solution(1165423933094130259)
XLA Ops:
  0.6 24.9 %shard_map.104 = (f32[128,512]{1,0:T(8,128)S(1)}, f32[128,512]{1,0:T(8,128)S(1)}) custom-call(f32[512,128]{1,0:T(8,128)} %right_hbm.1, f32[1,512]{1,0:T(1,128)} %bitcast.2, f32[8,512]{1,0:T(8,128)} %values_hbm.1, s32[8,512]{1,0:T(8,128)} %columns_hbm.1, bf16[1,1024,1024]{2,1,0:T(8,128)(2,1)} %inverse_hbm.1, s32[1,4,128]{2,1,0:T(4,128)} %list_hbm.1, ...), custom_call_target="tpu_custom_call" | custom-call | tf_op jit(solution)/shard_map/pallas_call | solution.py:267
  25.6 0.9 %shard_map.105 = (f32[512,128]{1,0:T(8,128)}, f32[512,128]{1,0:T(8,128)}) custom-call(f32[128,512]{1,0:T(8,128)S(1)} %get-tuple-element.4.solution_in, f32[128,512]{1,0:T(8,128)S(1)} %get-tuple-element.5.residual_in), custom_call_target="tpu_custom_call" | custom-call | tf_op jit(solution)/shard_map/pallas_call | solution.py:301

commit v4 on v3

--- a/solution.py
+++ b/solution.py
@@ -53,6 +53,8 @@
     coupling,
     send,
     recv,
+    ahead,
+    held,
     load_sem,
     send_sem,
     recv_sem,
@@ -200,14 +202,17 @@
             inverse_denominator = 1.0 / denominator
             build_coupling(0, total // 2)
             loads[7].wait()
-        term_ghost = [dot_nt(x, inverse[own:, :own]) for x in half]
-        term_own = [dot_nt(x, inverse[:own, :own]) for x in half]
+        for part in parts:
+            ahead[part] = dot_nt(half[part], inverse[own:, :own])
+        for part in parts:
+            held[part] = dot_nt(half[part], inverse[:own, :own])
         ghosts = [None] * PARTS
         for part in parts:
             ghosts[part] = finish(stage, part)
-            whole = term_ghost[part] + dot_nt(ghosts[part], inverse[own:, own:])
+            whole = ahead[part] + dot_nt(ghosts[part], inverse[own:, own:])
             start(stage + 1, part, lambda lanes: whole[:, lanes])
-        term_own = [own_weight * (term_own[part] + dot_nt(ghosts[part], inverse[:own, own:])) for part in parts]
+        for part in parts:
+            held[part] = own_weight * (held[part] + dot_nt(ghosts[part], inverse[:own, own:]))
         if iteration == 0:
             build_coupling(total // 2, total)
         else:
@@ -215,7 +220,7 @@
         for part in parts:
             returned = finish(stage + 1, part)
             weighted = (weight * returned.astype(F32)).astype(BF16)
-            update = (term_own[part] + dot_nt(weighted, pick[...])) * inverse_denominator
+            update = (held[part] + dot_nt(weighted, pick[...])) * inverse_denominator
             if iteration == 0:
                 direction[part] = update * (1.0 / center)
             else:
@@ -227,12 +232,12 @@
             ratio = ratio_next
         for part in parts:
             solution[part] = direction[part] if iteration == 0 else solution[part] + direction[part]
-            residual[part] = residual[part] - diag * direction[part] - dot_nn(half[part], coupling[:own, :])
-            if iteration == ITERS - 1:
-                solution_ref[part * rows : (part + 1) * rows, :] = solution[part]
+            held[part] = residual[part] - diag * direction[part] - dot_nn(half[part], coupling[:own, :])
+        if iteration == ITERS - 1:
+            solution_ref[...] = jnp.transpose(jnp.concatenate(solution, axis=0))
         for part in parts:
             ghosts[part] = finish(stage + 2, part)
-            residual[part] = residual[part] - dot_nn(ghosts[part], coupling[own:, :])
+            residual[part] = held[part] - dot_nn(ghosts[part], coupling[own:, :])
             if iteration < ITERS - 1:
                 half[part] = residual[part].astype(BF16)
                 whole = dot_nn(half[part], pick[...])
@@ -250,9 +255,17 @@
                     copy(stage, part, k, k ^ 1).wait_send()
 
 
-def flip(solution_in, residual_in, solution_ref, residual_ref):
-    solution_ref[...] = jnp.transpose(solution_in[...])
-    residual_ref[...] = jnp.transpose(residual_in[...])
+def write_out(solution_in, residual_in, solution_hbm, residual_hbm, flipped, sems):
+    own = residual_in.shape[1]
+    copies = [pltpu.make_async_copy(solution_in, solution_hbm, sems.at[0])]
+    copies[0].start()
+    for i in range(own // LANES):
+        lanes = slice(i * LANES, (i + 1) * LANES)
+        flipped[lanes, :] = jnp.transpose(residual_in[:, lanes])
+        copies.append(pltpu.make_async_copy(flipped.at[lanes], residual_hbm.at[lanes], sems.at[1 + i]))
+        copies[-1].start()
+    for copy in copies:
+        copy.wait()
 
 
 def per_device(n_x, n_y, right_side, prec_diag, prec_values, prec_columns, inverse, send_list, send_count, own_weight, copy_weight):
@@ -262,11 +275,11 @@
     rounds = 3 * ITERS
     vmem = pl.BlockSpec(memory_space=pltpu.VMEM)
     hbm = pl.BlockSpec(memory_space=pltpu.HBM)
-    field = pltpu.VMEM((width, own), F32)
+    fields = (pltpu.VMEM((own, width), F32), pltpu.VMEM((width, own), F32))
     out = jax.ShapeDtypeStruct((own, width), F32)
-    flipped = pl.pallas_call(
+    results = pl.pallas_call(
         functools.partial(kernel, n_x, n_y),
-        out_shape=(field, field),
+        out_shape=fields,
         in_specs=[hbm] * 6 + [pl.BlockSpec(memory_space=pltpu.SMEM)] + [hbm] * 2,
         out_specs=(vmem, vmem),
         scratch_shapes=[
@@ -282,6 +295,8 @@
             pltpu.VMEM((total, own), BF16),
             pltpu.VMEM((rounds, PARTS, 4, width // PARTS, slots), BF16),
             pltpu.VMEM((rounds, PARTS, 4, width // PARTS, slots), BF16),
+            pltpu.VMEM((PARTS, width // PARTS, 4 * slots), F32),
+            pltpu.VMEM((PARTS, width // PARTS, own), F32),
             pltpu.SemaphoreType.DMA((8,)),
             pltpu.SemaphoreType.DMA((2, PARTS, 4)),
             pltpu.SemaphoreType.DMA((2, PARTS, 4)),
@@ -299,12 +314,13 @@
         copy_weight,
     )
     return pl.pallas_call(
-        flip,
+        write_out,
         out_shape=(out, out),
         in_specs=[vmem, vmem],
-        out_specs=(vmem, vmem),
+        out_specs=(hbm, hbm),
+        scratch_shapes=[pltpu.VMEM((own, width), F32), pltpu.SemaphoreType.DMA((1 + own // LANES,))],
         compiler_params=pltpu.CompilerParams(vmem_limit_bytes=16 * 2**20),
-    )(*flipped)
+    )(*results)
 
 
 def solution(mesh):

time: 26.7 us -> 26.2 us (0.981)
  Pallas kernels: 25.9 us -> 25.4 us
    pallas_call x2, Pallas kernels: 25.9 us -> 25.4 us  [the longest x1 24.5 us: per_device(): pl.pallas_call(functools.partial(kernel, n_x, n_y), out_shape=fields, in_...]
where the time goes in v4:
time: 26.2 us; the launch traced here: 26 us
  Pallas kernels  25.4 us (97%)
  between operations  0.64 us (2%)
    pallas_call x1, Pallas kernels, per_device(): pl.pallas_call(functools.partial(kernel, n_x, n_y), out_shape=fields, in_...  24.5 us
    pallas_call x1, Pallas kernels, per_device(): pl.pallas_call(write_out, out_shape=(out, out), in_specs=[vmem, vmem], ou...  0.84 us

profile of v4, /device:TPU:1, one launch (start us, length us, event | category | flops | bytes accessed | tf_op | source)
XLA Modules:
  0.0 26.0 jit_solution(5046900466761418461)
XLA Ops:
  0.6 24.5 %shard_map.104 = (f32[512,128]{1,0:T(8,128)S(1)}, f32[128,512]{1,0:T(8,128)S(1)}) custom-call(f32[512,128]{1,0:T(8,128)} %right_hbm.1, f32[1,512]{1,0:T(1,128)} %bitcast.2, f32[8,512]{1,0:T(8,128)} %values_hbm.1, s32[8,512]{1,0:T(8,128)} %columns_hbm.1, bf16[1,1024,1024]{2,1,0:T(8,128)(2,1)} %inverse_hbm.1, s32[1,4,128]{2,1,0:T(4,128)} %list_hbm.1, ...), custom_call_target="tpu_custom_call" | custom-call | tf_op jit(solution)/shard_map/pallas_call | solution.py:280
  25.2 0.8 %shard_map.105 = (f32[512,128]{1,0:T(8,128)}, f32[512,128]{1,0:T(8,128)}) custom-call(f32[512,128]{1,0:T(8,128)S(1)} %get-tuple-element.4.solution_in, f32[128,512]{1,0:T(8,128)S(1)} %get-tuple-element.5.residual_in), custom_call_target="tpu_custom_call" | custom-call | tf_op jit(solution)/shard_map/pallas_call | solution.py:316

commit v5 on v4

--- a/solution.py
+++ b/solution.py
@@ -36,7 +36,7 @@
     columns_hbm,
     inverse_hbm,
     list_hbm,
-    count_ref,
+    count_hbm,
     own_hbm,
     copy_hbm,
     solution_ref,
@@ -46,6 +46,7 @@
     values_ref,
     columns_ref,
     list_ref,
+    count_ref,
     own_ref,
     copy_ref,
     inverse,
@@ -80,6 +81,7 @@
         pltpu.make_async_copy(source, place, load_sem.at[i])
         for i, (source, place) in enumerate(
             (
+                (count_hbm, count_ref),
                 (list_hbm.at[0], list_ref),
                 (right_hbm, right_ref),
                 (copy_hbm.at[0], copy_ref),
@@ -94,6 +96,7 @@
     for load in loads:
         load.start()
     loads[0].wait()
+    loads[1].wait()
     slot_id = lax.broadcasted_iota(jnp.int32, (1, slots), 1)
     node_id = lax.broadcasted_iota(jnp.int32, (own, slots), 0)
     for k in range(4):
@@ -101,7 +104,7 @@
         chosen = jnp.where(filled, list_ref[k : k + 1, :], -1)
         pick[:, k * slots : (k + 1) * slots] = jnp.where(node_id == chosen, 1.0, 0.0).astype(BF16)
 
-    loads[1].wait()
+    loads[2].wait()
     field = jnp.transpose(right_ref[...])
     rows = field.shape[0] // PARTS
     parts = range(PARTS)
@@ -183,7 +186,7 @@
     stage = 0
     for iteration in range(ITERS):
         if iteration == 0:
-            for load in loads[2:7]:
+            for load in loads[3:8]:
                 load.wait()
             diag = diag_ref[...]
             own_weight = own_ref[...]
@@ -201,7 +204,7 @@
             denominator = own_weight + (spread_weight[0:1] + spread_weight[16:17] + spread_weight[32:33])
             inverse_denominator = 1.0 / denominator
             build_coupling(0, total // 2)
-            loads[7].wait()
+            loads[8].wait()
         for part in parts:
             ahead[part] = dot_nt(half[part], inverse[own:, :own])
         for part in parts:
@@ -280,7 +283,7 @@
     results = pl.pallas_call(
         functools.partial(kernel, n_x, n_y),
         out_shape=fields,
-        in_specs=[hbm] * 6 + [pl.BlockSpec(memory_space=pltpu.SMEM)] + [hbm] * 2,
+        in_specs=[hbm] * 9,
         out_specs=(vmem, vmem),
         scratch_shapes=[
             pltpu.VMEM(right_side.shape, F32),
@@ -288,6 +291,7 @@
             pltpu.VMEM(prec_values.shape, F32),
             pltpu.VMEM(prec_columns.shape, jnp.int32),
             pltpu.VMEM((4, slots), jnp.int32),
+            pltpu.SMEM((1, 4), jnp.int32),
             pltpu.VMEM((1, own), F32),
             pltpu.VMEM((4, slots), F32),
             pltpu.VMEM((total, total), BF16),
@@ -297,7 +301,7 @@
             pltpu.VMEM((rounds, PARTS, 4, width // PARTS, slots), BF16),
             pltpu.VMEM((PARTS, width // PARTS, 4 * slots), F32),
             pltpu.VMEM((PARTS, width // PARTS, own), F32),
-            pltpu.SemaphoreType.DMA((8,)),
+            pltpu.SemaphoreType.DMA((9,)),
             pltpu.SemaphoreType.DMA((2, PARTS, 4)),
             pltpu.SemaphoreType.DMA((2, PARTS, 4)),
         ],

time: 26.2 us -> 25.5 us (0.973)
  Pallas kernels: 25.4 us -> 24.8 us
    pallas_call x1, Pallas kernels: 24.5 us -> 23.9 us  [per_device(): pl.pallas_call(functools.partial(kernel, n_x, n_y), out_shape=fields, in_...]
where the time goes in v5:
time: 25.5 us; the launch traced here: 25.4 us
  Pallas kernels  24.8 us (97%)
  between operations  0.64 us (3%)
    pallas_call x1, Pallas kernels, per_device(): pl.pallas_call(functools.partial(kernel, n_x, n_y), out_shape=fields, in_...  23.9 us
    pallas_call x1, Pallas kernels, per_device(): pl.pallas_call(write_out, out_shape=(out, out), in_specs=[vmem, vmem], ou...  0.84 us

profile of v5, /device:TPU:1, one launch (start us, length us, event | category | flops | bytes accessed | tf_op | source)
XLA Modules:
  0.0 25.4 jit_solution(13405769080748635277)
XLA Ops:
  0.6 23.9 %shard_map.104 = (f32[512,128]{1,0:T(8,128)S(1)}, f32[128,512]{1,0:T(8,128)S(1)}) custom-call(f32[512,128]{1,0:T(8,128)} %right_hbm.1, f32[1,512]{1,0:T(1,128)} %bitcast.2, f32[8,512]{1,0:T(8,128)} %values_hbm.1, s32[8,512]{1,0:T(8,128)} %columns_hbm.1, bf16[1,1024,1024]{2,1,0:T(8,128)(2,1)} %inverse_hbm.1, s32[1,4,128]{2,1,0:T(4,128)} %list_hbm.1, ...), custom_call_target="tpu_custom_call" | custom-call | tf_op jit(solution)/shard_map/pallas_call | solution.py:283
  24.6 0.8 %shard_map.105 = (f32[512,128]{1,0:T(8,128)}, f32[512,128]{1,0:T(8,128)}) custom-call(f32[512,128]{1,0:T(8,128)S(1)} %get-tuple-element.4.solution_in, f32[128,512]{1,0:T(8,128)S(1)} %get-tuple-element.5.residual_in), custom_call_target="tpu_custom_call" | custom-call | tf_op jit(solution)/shard_map/pallas_call | solution.py:320
